TPU v7x, 32 devices: a whole 2x2x4 slice. The times are simulated.
32 devices in a mesh: gx: 8 (over z, y), ha: 4 (over x, core).
Axes of the slice: x: 2, y: 2, z: 4, core: 2. Of those that a mesh axis runs over, the one named last changes fastest.
Arguments:
- value_field: float32 [8, 32, 16, 16], P('ha', None, 'gx'), may hold values from -6 to 6
- avoid_field: float32 [8, 32, 16, 16], P('ha', None, 'gx'), may hold values from -6 to 6
- sample_adjoint: float32 [8, 4, 8, 128], P('gx', 'ha'), may hold values from -6 to 6
- offset_y: float32 [8, 4, 8, 128], P('gx', 'ha'), may hold values from 0 to 1
- offset_s: float32 [8, 4, 8, 128], P('gx', 'ha'), may hold values from 0 to 1
- start_xy: int32 [8, 4, 8, 128], P('gx', 'ha'), may hold values from 0 to 30, as said below
- start_hs: int32 [8, 4, 8, 128], P('gx', 'ha'), may hold values from 0 to 62, as said below
- send_counts: int32 [8, 4, 8], P('gx', 'ha'), may hold values from 16 to 128, as said below
Outputs:
- next_value: float32 [8, 32, 16, 16], P('ha', None, 'gx')
- value_grad: float32 [8, 32, 16, 16], P('ha', None, 'gx')
- avoid_grad: float32 [8, 32, 16, 16], P('ha', None, 'gx')
Inputs may be any that keep to these rules, and one draw needn't show every extreme that they name: `start_xy`: the y cell of a start is at most 14. `start_hs`: the speed cell of a start is at most 30. `send_counts`: the live slots of a row are its first ones. For each index along ha, one owner drawn from the seed gets all 128 slots live from every sender.
All inputs are finite; a program needn't handle non-finite values.
Results may differ from a plain program's by a relative error of at most 0.00002.
Values sent between devices are 32-bit elements; how exact they have to be, the bound alone decides.
A program may use at most 64 MiB of HBM per device.

v0:
```python
import math
import jax
import jax.numpy as jnp
from jax import lax
from jax.sharding import PartitionSpec as P

TIME_STEP = 0.3
SHARPNESS = 2.0
SOFTENING = 0.1
TURN_RATE = 0.5
ACCELERATION = 0.3
SLOWEST = 0.2
SPEED_RANGE = 0.8
FASTEST = 1.0


def with_halo(block, sides, width):
    for axis, dim in sides:
        count = lax.axis_size(axis)
        forward = [(i, i + 1) for i in range(count - 1)]
        forward.append((count - 1, 0))
        backward = [(target, source) for source, target in forward]
        low = lax.ppermute(
            lax.slice_in_dim(block, block.shape[dim] - width, None, axis=dim), axis, forward
        )
        high = lax.ppermute(lax.slice_in_dim(block, 0, width, axis=dim), axis, backward)
        block = jnp.concatenate([low, block, high], axis=dim)
    return block


def smooth_abs(slope_value):
    return jnp.sqrt(slope_value * slope_value + SOFTENING * SOFTENING)


def edge_neighbours(grid_field, along_dim):
    length = grid_field.shape[along_dim]
    first_plane = lax.slice_in_dim(grid_field, 0, 1, axis=along_dim)
    last_plane = lax.slice_in_dim(grid_field, length - 1, length, axis=along_dim)
    upper_cells = jnp.concatenate(
        [lax.slice_in_dim(grid_field, 1, length, axis=along_dim), last_plane], along_dim
    )
    lower_cells = jnp.concatenate(
        [first_plane, lax.slice_in_dim(grid_field, 0, length - 1, axis=along_dim)], along_dim
    )
    return (upper_cells, lower_cells)


def linear_term(grid_field, upper_cells, lower_cells, factor):
    return (
        factor * (upper_cells - lower_cells) * 0.5
        - FASTEST * (upper_cells - 2.0 * grid_field + lower_cells) * 0.5
    )


def turn_term(grid_field, upper_cells, lower_cells, turn_rate):
    return turn_rate * smooth_abs(0.5 * (upper_cells - lower_cells)) - turn_rate * 0.5 * (
        upper_cells - 2.0 * grid_field + lower_cells
    )


def coefficients(head_index, total_heads, speeds):
    heading_angle = 2.0 * math.pi / total_heads * head_index.astype(jnp.float32)
    speed_cell = SLOWEST + SPEED_RANGE * jnp.arange(speeds, dtype=jnp.int32).astype(jnp.float32) / (
        speeds - 1
    )
    along_x = jnp.cos(heading_angle)[:, None, None, None] * speed_cell[None, :, None, None]
    along_y = jnp.sin(heading_angle)[:, None, None, None] * speed_cell[None, :, None, None]
    return (along_x, along_y)


def to_columns(grid_field):
    return jnp.swapaxes(
        lax.all_to_all(grid_field, "gx", split_axis=3, concat_axis=2, tiled=True), 2, 3
    )


def from_columns(grid_field):
    return lax.all_to_all(
        jnp.swapaxes(grid_field, 2, 3), "gx", split_axis=2, concat_axis=3, tiled=True
    )


def corner_weights(weight, offset_rows, offset_speed):
    return [
        weight * (1.0 - offset_rows) * (1.0 - offset_speed),
        weight * offset_rows * (1.0 - offset_speed),
        weight * (1.0 - offset_rows) * offset_speed,
        weight * offset_rows * offset_speed,
    ]


def on_device(
    value_field, avoid_field, sample_adjoint, offset_y, offset_s, start_xy, start_hs, send_counts
):
    head_count, speeds, row_count, line_count = value_field.shape
    groups = lax.axis_size("gx")
    slot_count = sample_adjoint.shape[3]
    head_index = lax.axis_index("ha") * head_count + jnp.arange(head_count, dtype=jnp.int32)
    along_x, along_y = coefficients(head_index, head_count * lax.axis_size("ha"), speeds)
    padded = with_halo(value_field, (("ha", 0),), 1)
    ahead_plane = padded[2:]
    behind = padded[:-2]
    slope_turn = 0.5 * (ahead_plane - behind)
    turning = TURN_RATE * smooth_abs(slope_turn) - TURN_RATE * 0.5 * (
        ahead_plane - 2.0 * value_field + behind
    )

    def local_terms(grid_field):
        upper_cells, lower_cells = edge_neighbours(grid_field, 3)
        summed = linear_term(grid_field, upper_cells, lower_cells, along_y)
        upper_cells, lower_cells = edge_neighbours(grid_field, 1)
        return summed + turn_term(grid_field, upper_cells, lower_cells, ACCELERATION)

    local_part, local_back = jax.vjp(local_terms, value_field)

    def line_term(grid_field):
        upper_cells, lower_cells = edge_neighbours(grid_field, 3)
        return linear_term(grid_field, upper_cells, lower_cells, along_x)

    across, line_back = jax.vjp(line_term, to_columns(value_field))
    across = from_columns(across)
    hamilton = across + local_part + turning
    relaxed = value_field - TIME_STEP * hamilton
    excess = SHARPNESS * (relaxed - avoid_field)
    next_value = avoid_field + jax.nn.softplus(excess) / SHARPNESS
    blend_share = jax.nn.sigmoid(excess)
    counts = send_counts.reshape(groups)
    live_slot = jnp.arange(slot_count, dtype=jnp.int32)[None, :] < counts[:, None]
    weight = jnp.where(live_slot, sample_adjoint.reshape(groups, slot_count), 0.0)
    offset_rows = offset_y.reshape(groups, slot_count)
    offset_speed = offset_s.reshape(groups, slot_count)
    cell_rows = start_xy.reshape(groups, slot_count)
    states = start_hs.reshape(groups, slot_count)
    payload = jnp.concatenate(corner_weights(weight, offset_rows, offset_speed), axis=1)
    payload, cell_rows, states = (
        lax.all_to_all(payload, "gx", split_axis=0, concat_axis=0, tiled=True),
        lax.all_to_all(cell_rows, "gx", split_axis=0, concat_axis=0, tiled=True),
        lax.all_to_all(states, "gx", split_axis=0, concat_axis=0, tiled=True),
    )
    pieces = jnp.split(payload, 4, axis=1)
    plane = row_count * line_count
    flat_index = states * plane + cell_rows
    cell_index = jnp.concatenate(
        [flat_index, flat_index + 1, flat_index + plane, flat_index + plane + 1], axis=0
    )
    deposit_sum = jnp.zeros((head_count * speeds * plane,), jnp.float32)
    deposit_sum = deposit_sum.at[cell_index.reshape(-1)].add(
        jnp.concatenate(pieces, axis=0).reshape(-1)
    )
    adjoint = deposit_sum.reshape(value_field.shape)
    avoid_grad = adjoint * (1.0 - blend_share)
    carried = adjoint * blend_share
    pull_turn = carried * TURN_RATE * slope_turn / smooth_abs(slope_turn)
    stacked = with_halo(jnp.stack([carried, pull_turn]), (("ha", 1),), 1)
    back_turn = 0.5 * (stacked[1, :-2] - stacked[1, 2:]) - TURN_RATE * 0.5 * (
        stacked[0, 2:] - 2.0 * carried + stacked[0, :-2]
    )
    back_local = local_back(carried)[0]
    back_across = from_columns(line_back(to_columns(carried))[0])
    value_grad = carried - TIME_STEP * (back_across + back_local + back_turn)
    return (next_value, value_grad, avoid_grad)


def solution(mesh):
    in_specs = (
        P("ha", None, "gx", None),
        P("ha", None, "gx", None),
        P("gx", "ha", None, None),
        P("gx", "ha", None, None),
        P("gx", "ha", None, None),
        P("gx", "ha", None, None),
        P("gx", "ha", None, None),
        P("gx", "ha", None),
    )
    out_specs = (P("ha", None, "gx", None), P("ha", None, "gx", None), P("ha", None, "gx", None))
    return jax.shard_map(
        on_device, mesh=mesh, in_specs=in_specs, out_specs=out_specs, check_vma=False
    )
```

profile of v0, /device:TPU:0, one launch (start us, length us, event | category | flops | bytes accessed | tf_op | source)
XLA Modules:
  0.0 99.8 jit_solution(10327407511817762513)
XLA Ops:
  0.6 7.3 %all-to-all-start.2 = ((s32[8,1,128]{2,1,0:T(1,128)}), s32[8,1,128]{2,1,0:T(1,128)S(1)}, u32[]{:S(2)}, u32[]{:S(2)}) async-start(s32[8,1,128]{2,1,0:T(1,128)} %bitcast.167), calls=%async_computation.2 | async-start | bytes 8192 | tf_op jit(solution)/shard_map/all_to_all | solution.py:138
  7.9 0.8 fusion.40
  8.7 0.7 collective-permute-start
  10.5 3.9 %all-to-all-done.2 = s32[8,1,128]{2,1,0:T(1,128)S(1)} async-done(((s32[8,1,128]{2,1,0:T(1,128)}), s32[8,1,128]{2,1,0:T(1,128)S(1)}, u32[]{:S(2)}, u32[]{:S(2)}) %all-to-all-start.2) | async-done | bytes 4128 | tf_op jit(solution)/shard_map/all_to_all | solution.py:138
  14.3 3.3 %all-to-all-start.3 = ((s32[8,1,128]{2,1,0:T(1,128)}), s32[8,1,128]{2,1,0:T(1,128)S(1)}, u32[]{:S(2)}, u32[]{:S(2)}) async-start(s32[8,1,128]{2,1,0:T(1,128)} %bitcast.11), calls=%async_computation.3 | async-start | bytes 8192 | tf_op jit(solution)/shard_map/all_to_all | solution.py:137
  17.7 0.6 all_to_all.84
  18.3 0.7 reshape.163
  19.0 5.0 %all-to-all-done.3 = s32[8,1,128]{2,1,0:T(1,128)S(1)} async-done(((s32[8,1,128]{2,1,0:T(1,128)}), s32[8,1,128]{2,1,0:T(1,128)S(1)}, u32[]{:S(2)}, u32[]{:S(2)}) %all-to-all-start.3) | async-done | bytes 4128 | tf_op jit(solution)/shard_map/all_to_all | solution.py:137
  24.0 3.3 %all-to-all-start = ((f32[8,1,256]{2,1,0:T(1,128)}), f32[8,1,256]{2,1,0:T(1,128)S(1)}, u32[]{:S(2)}, u32[]{:S(2)}) async-start(f32[8,1,256]{2,1,0:T(1,128)} %reshape.163), calls=%async_computation | async-start | bytes 16384 | tf_op jit(solution)/shard_map/all_to_all | solution.py:73
  27.4 6.4 %all-to-all-done = f32[8,1,256]{2,1,0:T(1,128)S(1)} async-done(((f32[8,1,256]{2,1,0:T(1,128)}), f32[8,1,256]{2,1,0:T(1,128)S(1)}, u32[]{:S(2)}, u32[]{:S(2)}) %all-to-all-start) | async-done | bytes 8224 | tf_op jit(solution)/shard_map/all_to_all | solution.py:73
  33.8 3.3 %all-to-all-start.4 = ((f32[8,1,512]{2,1,0:T(1,128)}), f32[8,1,512]{2,1,0:T(1,128)S(1)}, u32[]{:S(2)}, u32[]{:S(2)}) async-start(f32[8,1,512]{2,1,0:T(1,128)} %all_to_all.84), calls=%async_computation.4 | async-start | bytes 32768 | tf_op jit(solution)/shard_map/all_to_all | solution.py:136
  37.7 0.7 reduce
  38.6 0.7 reshape.165
  39.3 4.3 %all-to-all-done.4 = f32[8,1,512]{2,1,0:T(1,128)S(1)} async-done(((f32[8,1,512]{2,1,0:T(1,128)}), f32[8,1,512]{2,1,0:T(1,128)S(1)}, u32[]{:S(2)}, u32[]{:S(2)}) %all-to-all-start.4) | async-done | bytes 16416 | tf_op jit(solution)/shard_map/all_to_all | solution.py:136
  43.6 3.3 %all-to-all-start.1 = ((f32[8,1,256]{2,1,0:T(1,128)}), f32[8,1,256]{2,1,0:T(1,128)S(1)}, u32[]{:S(2)}, u32[]{:S(2)}) async-start(f32[8,1,256]{2,1,0:T(1,128)} %reshape.165), calls=%async_computation.1 | async-start | bytes 16384 | tf_op jit(solution)/shard_map/all_to_all | solution.py:78
  47.0 22.0 %scatter_custom_fusion = f32[2048]{0:T(1024)S(1)} fusion(s32[4096]{0:T(1024)S(1)} %bitcast.166, f32[4096]{0:T(1024)S(1)} %maximum_bitcast_fusion, f32[]{:T(128)} %constant.18.clone.1), kind=kCustom, calls=%fused_computation.78 | custom fusion | flops 4096 | bytes 8196 | tf_op jit(solution)/shard_map/scatter-add | solution.py:147
  69.2 0.7 reduce.1
  70.1 0.7 copy-done.1
  70.8 0.8 subtract_multiply_fusion
  71.6 0.7 negate_add_fusion.1
  72.3 0.7 reshape.167
  73.0 6.0 %all-to-all-start.5 = ((f32[8,1,256]{2,1,0:T(1,128)}), f32[8,1,256]{2,1,0:T(1,128)S(1)}, u32[]{:S(2)}, u32[]{:S(2)}) async-start(f32[8,1,256]{2,1,0:T(1,128)} %reshape.167), calls=%async_computation.5 | async-start | bytes 16384 | tf_op jit(solution)/shard_map/all_to_all | solution.py:73
  79.0 6.5 %all-to-all-done.5 = f32[8,1,256]{2,1,0:T(1,128)S(1)} async-done(((f32[8,1,256]{2,1,0:T(1,128)}), f32[8,1,256]{2,1,0:T(1,128)S(1)}, u32[]{:S(2)}, u32[]{:S(2)}) %all-to-all-start.5) | async-done | bytes 8224 | tf_op jit(solution)/shard_map/all_to_all | solution.py:73
  85.4 0.7 reduce.2
  86.3 0.6 copy-done.5
  87.1 0.7 reshape.169
  87.8 3.3 %all-to-all-start.6 = ((f32[8,1,256]{2,1,0:T(1,128)}), f32[8,1,256]{2,1,0:T(1,128)S(1)}, u32[]{:S(2)}, u32[]{:S(2)}) async-start(f32[8,1,256]{2,1,0:T(1,128)} %reshape.169), calls=%async_computation.6 | async-start | bytes 16384 | tf_op jit(solution)/shard_map/all_to_all | solution.py:78
  91.2 1.7 %collective-permute-start.3 = (f32[2,1,32,2,16]{2,4,3,1,0:T(8,128)S(1)}, f32[2,1,32,2,16]{2,4,3,1,0:T(8,128)S(1)}, u32[]{:S(2)}, u32[]{:S(2)}) collective-permute-start(f32[2,1,32,2,16]{2,4,3,1,0:T(8,128)S(1)} %get-tuple-element.11), channel_id=1, source_target_pairs={{1,0},{2,1},{3,2},{0,3},{5,4},{6,5},{7,6},{4,7},{9,8},{10,9},{11,1... | collective-permute-start | bytes 24584 | tf_op jit(solution)/shard_map/ppermute | solution.py:26
  93.1 4.5 %all-to-all-done.6 = f32[8,1,256]{2,1,0:T(1,128)S(1)} async-done(((f32[8,1,256]{2,1,0:T(1,128)}), f32[8,1,256]{2,1,0:T(1,128)S(1)}, u32[]{:S(2)}, u32[]{:S(2)}) %all-to-all-start.6) | async-done | bytes 8224 | tf_op jit(solution)/shard_map/all_to_all | solution.py:78
  97.6 0.7 reduce.3
  98.5 0.6 copy-done.7
  99.1 0.7 fusion.9
  (67 shorter events, 2.8 us)
Async XLA Ops:
  0.6 13.7 %all-to-all-start.2 = ((s32[8,1,128]{2,1,0:T(1,128)}), s32[8,1,128]{2,1,0:T(1,128)S(1)}, u32[]{:S(2)}, u32[]{:S(2)}) async-start(s32[8,1,128]{2,1,0:T(1,128)} %bitcast.167), calls=%async_computation.2 | async-start | bytes 8192 | tf_op jit(solution)/shard_map/all_to_all | solution.py:138
  7.9 1.5 %copy-start = (f32[2,32,2,16]{1,3,2,0:T(8,128)S(1)}, f32[2,32,2,16]{1,3,2,0:T(8,128)}, u32[]{:S(2)}) copy-start(f32[2,32,2,16]{1,3,2,0:T(8,128)} %param.8) | copy-start | bytes 24580
  8.7 61.4 %collective-permute-start = (f32[1,32,2,16]{1,3,2,0:T(8,128)S(1)}, f32[1,32,2,16]{1,3,2,0:T(8,128)S(1)}, u32[]{:S(2)}, u32[]{:S(2)}) collective-permute-start(f32[1,32,2,16]{1,3,2,0:T(8,128)S(1)} %get-tuple-element.34), channel_id=1, source_target_pairs={{1,0},{2,1},{3,2},{0,3},{5,4},{6,5},{7,6},{4,7},{9,8},{10,9},{11,1... | collective-permute-start | bytes 12296 | tf_op jit(solution)/shard_map/ppermute | solution.py:26
  9.4 60.7 %collective-permute-start.1 = (f32[1,32,2,16]{1,3,2,0:T(8,128)S(1)}, f32[1,32,2,16]{1,3,2,0:T(8,128)S(1)}, u32[]{:S(2)}, u32[]{:S(2)}) collective-permute-start(f32[1,32,2,16]{1,3,2,0:T(8,128)S(1)} %get-tuple-element.35), channel_id=1, source_target_pairs={{0,1},{1,2},{2,3},{3,0},{4,5},{5,6},{6,7},{7,4},{8,9},{9,10},{10,1... | collective-permute-start | bytes 12296 | tf_op jit(solution)/shard_map/ppermute | solution.py:23
  9.5 0.7 copy-start.4
  9.6 0.7 copy-start.3
  9.6 0.7 copy-start.2
  9.6 0.7 copy-start.6
  14.3 9.6 %all-to-all-start.3 = ((s32[8,1,128]{2,1,0:T(1,128)}), s32[8,1,128]{2,1,0:T(1,128)S(1)}, u32[]{:S(2)}, u32[]{:S(2)}) async-start(s32[8,1,128]{2,1,0:T(1,128)} %bitcast.11), calls=%async_computation.3 | async-start | bytes 8192 | tf_op jit(solution)/shard_map/all_to_all | solution.py:137
  24.0 9.8 %all-to-all-start = ((f32[8,1,256]{2,1,0:T(1,128)}), f32[8,1,256]{2,1,0:T(1,128)S(1)}, u32[]{:S(2)}, u32[]{:S(2)}) async-start(f32[8,1,256]{2,1,0:T(1,128)} %reshape.163), calls=%async_computation | async-start | bytes 16384 | tf_op jit(solution)/shard_map/all_to_all | solution.py:73
  33.8 9.9 %all-to-all-start.4 = ((f32[8,1,512]{2,1,0:T(1,128)}), f32[8,1,512]{2,1,0:T(1,128)S(1)}, u32[]{:S(2)}, u32[]{:S(2)}) async-start(f32[8,1,512]{2,1,0:T(1,128)} %all_to_all.84), calls=%async_computation.4 | async-start | bytes 32768 | tf_op jit(solution)/shard_map/all_to_all | solution.py:136
  43.6 25.6 %all-to-all-start.1 = ((f32[8,1,256]{2,1,0:T(1,128)}), f32[8,1,256]{2,1,0:T(1,128)S(1)}, u32[]{:S(2)}, u32[]{:S(2)}) async-start(f32[8,1,256]{2,1,0:T(1,128)} %reshape.165), calls=%async_computation.1 | async-start | bytes 16384 | tf_op jit(solution)/shard_map/all_to_all | solution.py:78
  70.1 0.8 copy-start.1
  73.0 12.5 %all-to-all-start.5 = ((f32[8,1,256]{2,1,0:T(1,128)}), f32[8,1,256]{2,1,0:T(1,128)S(1)}, u32[]{:S(2)}, u32[]{:S(2)}) async-start(f32[8,1,256]{2,1,0:T(1,128)} %reshape.167), calls=%async_computation.5 | async-start | bytes 16384 | tf_op jit(solution)/shard_map/all_to_all | solution.py:73
  86.3 0.7 copy-start.5
  87.8 9.8 %all-to-all-start.6 = ((f32[8,1,256]{2,1,0:T(1,128)}), f32[8,1,256]{2,1,0:T(1,128)S(1)}, u32[]{:S(2)}, u32[]{:S(2)}) async-start(f32[8,1,256]{2,1,0:T(1,128)} %reshape.169), calls=%async_computation.6 | async-start | bytes 16384 | tf_op jit(solution)/shard_map/all_to_all | solution.py:78
  91.1 7.3 %collective-permute-start.2 = (f32[2,1,32,2,16]{2,4,3,1,0:T(8,128)S(1)}, f32[2,1,32,2,16]{2,4,3,1,0:T(8,128)S(1)}, u32[]{:S(2)}, u32[]{:S(2)}) collective-permute-start(f32[2,1,32,2,16]{2,4,3,1,0:T(8,128)S(1)} %get-tuple-element.12), channel_id=1, source_target_pairs={{0,1},{1,2},{2,3},{3,0},{4,5},{5,6},{6,7},{7,4},{8,9},{9,10},{10,1... | collective-permute-start | bytes 24584 | tf_op jit(solution)/shard_map/ppermute | solution.py:23
  91.2 7.2 %collective-permute-start.3 = (f32[2,1,32,2,16]{2,4,3,1,0:T(8,128)S(1)}, f32[2,1,32,2,16]{2,4,3,1,0:T(8,128)S(1)}, u32[]{:S(2)}, u32[]{:S(2)}) collective-permute-start(f32[2,1,32,2,16]{2,4,3,1,0:T(8,128)S(1)} %get-tuple-element.11), channel_id=1, source_target_pairs={{1,0},{2,1},{3,2},{0,3},{5,4},{6,5},{7,6},{4,7},{9,8},{10,9},{11,1... | collective-permute-start | bytes 24584 | tf_op jit(solution)/shard_map/ppermute | solution.py:26
  98.5 0.7 copy-start.7
where the time goes:
time: 101 us; the launch traced here: 99.8 us
  starting transfers between devices  32.4 us (32%)
  waiting for transfers between devices  30.5 us (30%)
  other arithmetic  27.4 us (27%)
  local copies, waits for them, and re-layouts  8.55 us (8%)
  between operations  1.07 us (1%)
    scatter-add x1, other arithmetic, on_device(): deposit_sum.at[cell_index.reshape(-1)]  22 us
    all_to_all x2, waiting for transfers between devices, to_columns(): lax.all_to_all(grid_field, 'gx', split_axis=3, concat_axis=2, tiled=True)  12.9 us
    all_to_all x2, starting transfers between devices, to_columns(): lax.all_to_all(grid_field, 'gx', split_axis=3, concat_axis=2, tiled=True)  9.31 us
    all_to_all x1, starting transfers between devices, on_device(): lax.all_to_all(states, 'gx', split_axis=0, concat_axis=0, tiled=True)  7.29 us
    all_to_all x2, starting transfers between devices, from_columns(): lax.all_to_all(jnp.swapaxes(grid_field, 2, 3), 'gx', split_axis=2, concat...  6.67 us
    unnamed x26, local copies, waits for them, and re-layouts  5.85 us
    all_to_all x1, waiting for transfers between devices, on_device(): lax.all_to_all(cell_rows, 'gx', split_axis=0, concat_axis=0, tiled=True)  4.97 us
    all_to_all x2, waiting for transfers between devices, from_columns(): lax.all_to_all(jnp.swapaxes(grid_field, 2, 3), 'gx', split_axis=2, concat...  4.47 us
  transfers between devices with their start and end apart: 11, of which 6 were waited for; matrix products, arithmetic and copies ran while one was open for 28% of the time, Pallas kernels for 0%

commit v1 on v0

--- a/solution.py
+++ b/solution.py
@@ -70,7 +70,14 @@
 
 def to_columns(grid_field):
     return jnp.swapaxes(
-        lax.all_to_all(grid_field, "gx", split_axis=3, concat_axis=2, tiled=True), 2, 3
+        jnp.concatenate(
+            lax.all_to_all(
+                jnp.stack(jnp.split(grid_field, lax.axis_size("gx"), axis=3)), "gx", 0, 0
+            ),
+            axis=2,
+        ),
+        2,
+        3,
     )
 
 

time: 101 us -> 101 us (level)
    unnamed x26 -> x39, local copies, waits for them, and re-layouts: 5.85 us -> 5.97 us
where the time goes in v1:
time: 101 us; the launch traced here: 99.9 us
  starting transfers between devices  32.4 us (32%)
  waiting for transfers between devices  30.4 us (30%)
  other arithmetic  27.4 us (27%)
  local copies, waits for them, and re-layouts  8.68 us (9%)
  between operations  1.12 us (1%)
    scatter-add x1, other arithmetic, on_device(): deposit_sum.at[cell_index.reshape(-1)]  22 us
    all_to_all x2, waiting for transfers between devices, to_columns(): lax.all_to_all(jnp.stack(jnp.split(grid_field, lax.axis_size('gx'), axis=...  12.9 us
    all_to_all x2, starting transfers between devices, to_columns(): lax.all_to_all(jnp.stack(jnp.split(grid_field, lax.axis_size('gx'), axis=...  9.31 us
    all_to_all x1, starting transfers between devices, on_device(): lax.all_to_all(states, 'gx', split_axis=0, concat_axis=0, tiled=True)  7.29 us
    all_to_all x2, starting transfers between devices, from_columns(): lax.all_to_all(jnp.swapaxes(grid_field, 2, 3), 'gx', split_axis=2, concat...  6.67 us
    unnamed x39, local copies, waits for them, and re-layouts  5.97 us
    all_to_all x1, waiting for transfers between devices, on_device(): lax.all_to_all(cell_rows, 'gx', split_axis=0, concat_axis=0, tiled=True)  4.99 us
    all_to_all x2, waiting for transfers between devices, from_columns(): lax.all_to_all(jnp.swapaxes(grid_field, 2, 3), 'gx', split_axis=2, concat...  4.47 us
  transfers between devices with their start and end apart: 11, of which 6 were waited for; matrix products, arithmetic and copies ran while one was open for 28% of the time, Pallas kernels for 0%

profile of v1, /device:TPU:0, one launch (start us, length us, event | category | flops | bytes accessed | tf_op | source)
XLA Modules:
  0.0 99.9 jit_solution(9006966550618875637)
XLA Ops:
  0.6 7.3 %all-to-all-start.2 = ((s32[8,1,128]{2,1,0:T(1,128)}), s32[8,1,128]{2,1,0:T(1,128)S(1)}, u32[]{:S(2)}, u32[]{:S(2)}) async-start(s32[8,1,128]{2,1,0:T(1,128)} %bitcast.208), calls=%async_computation.2 | async-start | bytes 8192 | tf_op jit(solution)/shard_map/all_to_all | solution.py:145
  7.9 0.8 fusion.40
  8.7 0.7 collective-permute-start
  10.6 3.7 %all-to-all-done.2 = s32[8,1,128]{2,1,0:T(1,128)S(1)} async-done(((s32[8,1,128]{2,1,0:T(1,128)}), s32[8,1,128]{2,1,0:T(1,128)S(1)}, u32[]{:S(2)}, u32[]{:S(2)}) %all-to-all-start.2) | async-done | bytes 4128 | tf_op jit(solution)/shard_map/all_to_all | solution.py:145
  14.3 3.3 %all-to-all-start.3 = ((s32[8,1,128]{2,1,0:T(1,128)}), s32[8,1,128]{2,1,0:T(1,128)S(1)}, u32[]{:S(2)}, u32[]{:S(2)}) async-start(s32[8,1,128]{2,1,0:T(1,128)} %bitcast.17), calls=%async_computation.3 | async-start | bytes 8192 | tf_op jit(solution)/shard_map/all_to_all | solution.py:144
  17.6 0.6 all_to_all.61
  18.3 0.7 reshape.179
  19.0 5.0 %all-to-all-done.3 = s32[8,1,128]{2,1,0:T(1,128)S(1)} async-done(((s32[8,1,128]{2,1,0:T(1,128)}), s32[8,1,128]{2,1,0:T(1,128)S(1)}, u32[]{:S(2)}, u32[]{:S(2)}) %all-to-all-start.3) | async-done | bytes 4128 | tf_op jit(solution)/shard_map/all_to_all | solution.py:144
  24.0 3.3 %all-to-all-start = ((f32[8,1,256]{2,1,0:T(1,128)}), f32[8,1,256]{2,1,0:T(1,128)S(1)}, u32[]{:S(2)}, u32[]{:S(2)}) async-start(f32[8,1,256]{2,1,0:T(1,128)} %reshape.179), calls=%async_computation | async-start | bytes 16384 | tf_op jit(solution)/shard_map/all_to_all | solution.py:74
  27.4 6.4 %all-to-all-done = f32[8,1,256]{2,1,0:T(1,128)S(1)} async-done(((f32[8,1,256]{2,1,0:T(1,128)}), f32[8,1,256]{2,1,0:T(1,128)S(1)}, u32[]{:S(2)}, u32[]{:S(2)}) %all-to-all-start) | async-done | bytes 8224 | tf_op jit(solution)/shard_map/all_to_all | solution.py:74
  33.8 3.3 %all-to-all-start.4 = ((f32[8,1,512]{2,1,0:T(1,128)}), f32[8,1,512]{2,1,0:T(1,128)S(1)}, u32[]{:S(2)}, u32[]{:S(2)}) async-start(f32[8,1,512]{2,1,0:T(1,128)} %all_to_all.61), calls=%async_computation.4 | async-start | bytes 32768 | tf_op jit(solution)/shard_map/all_to_all | solution.py:143
  37.7 0.7 reduce
  38.6 0.7 reshape.181
  39.3 4.3 %all-to-all-done.4 = f32[8,1,512]{2,1,0:T(1,128)S(1)} async-done(((f32[8,1,512]{2,1,0:T(1,128)}), f32[8,1,512]{2,1,0:T(1,128)S(1)}, u32[]{:S(2)}, u32[]{:S(2)}) %all-to-all-start.4) | async-done | bytes 16416 | tf_op jit(solution)/shard_map/all_to_all | solution.py:143
  43.6 3.3 %all-to-all-start.1 = ((f32[8,1,256]{2,1,0:T(1,128)}), f32[8,1,256]{2,1,0:T(1,128)S(1)}, u32[]{:S(2)}, u32[]{:S(2)}) async-start(f32[8,1,256]{2,1,0:T(1,128)} %reshape.181), calls=%async_computation.1 | async-start | bytes 16384 | tf_op jit(solution)/shard_map/all_to_all | solution.py:85
  47.0 22.0 %scatter_custom_fusion = f32[2048]{0:T(1024)S(1)} fusion(s32[4096]{0:T(1024)S(1)} %bitcast.207, f32[4096]{0:T(1024)S(1)} %maximum_bitcast_fusion, f32[]{:T(128)} %constant.18.clone.1), kind=kCustom, calls=%fused_computation.102 | custom fusion | flops 4096 | bytes 8196 | tf_op jit(solution)/shard_map/scatter-add | solution.py:154
  69.2 0.7 reduce.1
  70.1 0.7 copy-done.1
  70.8 0.8 subtract_multiply_fusion
  71.6 0.7 negate_add_fusion.1
  72.3 0.7 reshape.183
  73.0 6.0 %all-to-all-start.5 = ((f32[8,1,256]{2,1,0:T(1,128)}), f32[8,1,256]{2,1,0:T(1,128)S(1)}, u32[]{:S(2)}, u32[]{:S(2)}) async-start(f32[8,1,256]{2,1,0:T(1,128)} %reshape.183), calls=%async_computation.5 | async-start | bytes 16384 | tf_op jit(solution)/shard_map/all_to_all | solution.py:74
  79.0 6.5 %all-to-all-done.5 = f32[8,1,256]{2,1,0:T(1,128)S(1)} async-done(((f32[8,1,256]{2,1,0:T(1,128)}), f32[8,1,256]{2,1,0:T(1,128)S(1)}, u32[]{:S(2)}, u32[]{:S(2)}) %all-to-all-start.5) | async-done | bytes 8224 | tf_op jit(solution)/shard_map/all_to_all | solution.py:74
  85.5 0.7 reduce.2
  86.4 0.6 copy-done.5
  87.2 0.7 reshape.185
  87.9 3.3 %all-to-all-start.6 = ((f32[8,1,256]{2,1,0:T(1,128)}), f32[8,1,256]{2,1,0:T(1,128)S(1)}, u32[]{:S(2)}, u32[]{:S(2)}) async-start(f32[8,1,256]{2,1,0:T(1,128)} %reshape.185), calls=%async_computation.6 | async-start | bytes 16384 | tf_op jit(solution)/shard_map/all_to_all | solution.py:85
  91.3 1.7 %collective-permute-start.3 = (f32[2,1,32,2,16]{2,4,3,1,0:T(8,128)S(1)}, f32[2,1,32,2,16]{2,4,3,1,0:T(8,128)S(1)}, u32[]{:S(2)}, u32[]{:S(2)}) collective-permute-start(f32[2,1,32,2,16]{2,4,3,1,0:T(8,128)S(1)} %get-tuple-element.11), channel_id=1, source_target_pairs={{1,0},{2,1},{3,2},{0,3},{5,4},{6,5},{7,6},{4,7},{9,8},{10,9},{11,1... | collective-permute-start | bytes 24584 | tf_op jit(solution)/shard_map/ppermute | solution.py:26
  93.2 4.5 %all-to-all-done.6 = f32[8,1,256]{2,1,0:T(1,128)S(1)} async-done(((f32[8,1,256]{2,1,0:T(1,128)}), f32[8,1,256]{2,1,0:T(1,128)S(1)}, u32[]{:S(2)}, u32[]{:S(2)}) %all-to-all-start.6) | async-done | bytes 8224 | tf_op jit(solution)/shard_map/all_to_all | solution.py:85
  97.7 0.7 reduce.3
  98.5 0.6 copy-done.7
  99.2 0.7 fusion.9
  (82 shorter events, 3.0 us)
Async XLA Ops:
  0.6 13.7 %all-to-all-start.2 = ((s32[8,1,128]{2,1,0:T(1,128)}), s32[8,1,128]{2,1,0:T(1,128)S(1)}, u32[]{:S(2)}, u32[]{:S(2)}) async-start(s32[8,1,128]{2,1,0:T(1,128)} %bitcast.208), calls=%async_computation.2 | async-start | bytes 8192 | tf_op jit(solution)/shard_map/all_to_all | solution.py:145
  7.9 1.5 %copy-start = (f32[2,32,2,16]{1,3,2,0:T(8,128)S(1)}, f32[2,32,2,16]{1,3,2,0:T(8,128)}, u32[]{:S(2)}) copy-start(f32[2,32,2,16]{1,3,2,0:T(8,128)} %param.8) | copy-start | bytes 24580
  8.7 61.4 %collective-permute-start = (f32[1,32,2,16]{1,3,2,0:T(8,128)S(1)}, f32[1,32,2,16]{1,3,2,0:T(8,128)S(1)}, u32[]{:S(2)}, u32[]{:S(2)}) collective-permute-start(f32[1,32,2,16]{1,3,2,0:T(8,128)S(1)} %get-tuple-element.34), channel_id=1, source_target_pairs={{1,0},{2,1},{3,2},{0,3},{5,4},{6,5},{7,6},{4,7},{9,8},{10,9},{11,1... | collective-permute-start | bytes 12296 | tf_op jit(solution)/shard_map/ppermute | solution.py:26
  9.4 60.7 %collective-permute-start.1 = (f32[1,32,2,16]{1,3,2,0:T(8,128)S(1)}, f32[1,32,2,16]{1,3,2,0:T(8,128)S(1)}, u32[]{:S(2)}, u32[]{:S(2)}) collective-permute-start(f32[1,32,2,16]{1,3,2,0:T(8,128)S(1)} %get-tuple-element.35), channel_id=1, source_target_pairs={{0,1},{1,2},{2,3},{3,0},{4,5},{5,6},{6,7},{7,4},{8,9},{9,10},{10,1... | collective-permute-start | bytes 12296 | tf_op jit(solution)/shard_map/ppermute | solution.py:23
  9.7 0.7 copy-start.4
  9.7 0.7 copy-start.3
  9.7 0.7 copy-start.2
  9.8 0.7 copy-start.6
  14.3 9.6 %all-to-all-start.3 = ((s32[8,1,128]{2,1,0:T(1,128)}), s32[8,1,128]{2,1,0:T(1,128)S(1)}, u32[]{:S(2)}, u32[]{:S(2)}) async-start(s32[8,1,128]{2,1,0:T(1,128)} %bitcast.17), calls=%async_computation.3 | async-start | bytes 8192 | tf_op jit(solution)/shard_map/all_to_all | solution.py:144
  24.0 9.8 %all-to-all-start = ((f32[8,1,256]{2,1,0:T(1,128)}), f32[8,1,256]{2,1,0:T(1,128)S(1)}, u32[]{:S(2)}, u32[]{:S(2)}) async-start(f32[8,1,256]{2,1,0:T(1,128)} %reshape.179), calls=%async_computation | async-start | bytes 16384 | tf_op jit(solution)/shard_map/all_to_all | solution.py:74
  33.8 9.9 %all-to-all-start.4 = ((f32[8,1,512]{2,1,0:T(1,128)}), f32[8,1,512]{2,1,0:T(1,128)S(1)}, u32[]{:S(2)}, u32[]{:S(2)}) async-start(f32[8,1,512]{2,1,0:T(1,128)} %all_to_all.61), calls=%async_computation.4 | async-start | bytes 32768 | tf_op jit(solution)/shard_map/all_to_all | solution.py:143
  43.6 25.6 %all-to-all-start.1 = ((f32[8,1,256]{2,1,0:T(1,128)}), f32[8,1,256]{2,1,0:T(1,128)S(1)}, u32[]{:S(2)}, u32[]{:S(2)}) async-start(f32[8,1,256]{2,1,0:T(1,128)} %reshape.181), calls=%async_computation.1 | async-start | bytes 16384 | tf_op jit(solution)/shard_map/all_to_all | solution.py:85
  70.1 0.8 copy-start.1
  73.0 12.5 %all-to-all-start.5 = ((f32[8,1,256]{2,1,0:T(1,128)}), f32[8,1,256]{2,1,0:T(1,128)S(1)}, u32[]{:S(2)}, u32[]{:S(2)}) async-start(f32[8,1,256]{2,1,0:T(1,128)} %reshape.183), calls=%async_computation.5 | async-start | bytes 16384 | tf_op jit(solution)/shard_map/all_to_all | solution.py:74
  86.4 0.7 copy-start.5
  87.9 9.8 %all-to-all-start.6 = ((f32[8,1,256]{2,1,0:T(1,128)}), f32[8,1,256]{2,1,0:T(1,128)S(1)}, u32[]{:S(2)}, u32[]{:S(2)}) async-start(f32[8,1,256]{2,1,0:T(1,128)} %reshape.185), calls=%async_computation.6 | async-start | bytes 16384 | tf_op jit(solution)/shard_map/all_to_all | solution.py:85
  91.2 7.3 %collective-permute-start.2 = (f32[2,1,32,2,16]{2,4,3,1,0:T(8,128)S(1)}, f32[2,1,32,2,16]{2,4,3,1,0:T(8,128)S(1)}, u32[]{:S(2)}, u32[]{:S(2)}) collective-permute-start(f32[2,1,32,2,16]{2,4,3,1,0:T(8,128)S(1)} %get-tuple-element.12), channel_id=1, source_target_pairs={{0,1},{1,2},{2,3},{3,0},{4,5},{5,6},{6,7},{7,4},{8,9},{9,10},{10,1... | collective-permute-start | bytes 24584 | tf_op jit(solution)/shard_map/ppermute | solution.py:23
  91.3 7.2 %collective-permute-start.3 = (f32[2,1,32,2,16]{2,4,3,1,0:T(8,128)S(1)}, f32[2,1,32,2,16]{2,4,3,1,0:T(8,128)S(1)}, u32[]{:S(2)}, u32[]{:S(2)}) collective-permute-start(f32[2,1,32,2,16]{2,4,3,1,0:T(8,128)S(1)} %get-tuple-element.11), channel_id=1, source_target_pairs={{1,0},{2,1},{3,2},{0,3},{5,4},{6,5},{7,6},{4,7},{9,8},{10,9},{11,1... | collective-permute-start | bytes 24584 | tf_op jit(solution)/shard_map/ppermute | solution.py:26
  98.5 0.7 copy-start.7
